TPU v7x, 512 devices: a whole 4x8x8 slice. The times are simulated.
512 devices in a mesh: row: 16 (over x, y_lo), col: 16 (over z, core), dp: 2 (over y_hi).
Axes of the slice: x: 4, y: 8 (y_hi: 2, y_lo: 4; y = y_hi * 4 + y_lo), z: 8, core: 2. Of those that a mesh axis runs over, the one named last changes fastest.
Arguments:
- grad_output: bfloat16 [2, 2048, 8192], P('dp', 'col', 'row'), may hold values from -0.09375 to 0.09375
- block_input: bfloat16 [2, 2048, 8192], P('dp', 'col', 'row'), may hold values from -6 to 6
- query_branch: bfloat16 [2, 2048, 8192], P('dp', 'row', 'col'), may hold values from -6 to 6
- key_branch: bfloat16 [2, 2048, 8192], P('dp', 'row', 'col'), may hold values from -6 to 6
- value_branch: bfloat16 [2, 2048, 8192], P('dp', 'row', 'col'), may hold values from -6 to 6
- out_weight: bfloat16 [8192, 8192], P('row', 'col'), may hold values from -0.0625 to 0.0625
- filters: float32 [512, 128], P('col'), may hold values from -0.5 to 0.5
Outputs:
- out_weight_grad: float32 [8192, 8192], P('row', 'col')
- value_weight_grad: float32 [8192, 8192], P('col', 'row')
- filter_grad: float32 [512, 128], P('col')
All inputs are finite; a program needn't handle non-finite values.
Results may differ from a plain program's by a relative error of at most 0.0029.
Values may be sent and summed in bfloat16 or wider, within the bound.
A program may use at most 128 MiB of HBM per device.

v0:
```python
import jax
import jax.numpy as jnp
from jax import lax
from jax.sharding import PartitionSpec as P

highest = lax.Precision.HIGHEST


def toeplitz(taps, tok_rows, causal):
    filter_len = taps.shape[1]
    out_pos = lax.broadcasted_iota(jnp.int32, (tok_rows, tok_rows + filter_len), 0)
    in_pos = lax.broadcasted_iota(jnp.int32, (tok_rows, tok_rows + filter_len), 1)
    lagged = out_pos + filter_len - in_pos if causal else in_pos - out_pos
    inside = (lagged >= 0) & (lagged < filter_len)
    picked = jnp.take(taps, jnp.clip(lagged, 0, filter_len - 1), axis=1)
    return jnp.where(inside[None], picked, 0.0)


def grouped_apply(table, signal, groups):
    blocks, extent, channels = signal.shape
    split = signal.reshape(blocks, extent, groups, channels // groups)
    result = jnp.einsum("gts,bsgc->btgc", table, split, precision=highest)
    return result.reshape(blocks, table.shape[1], channels)


def taps_partial(delta_mix, mixed_ext, groups, filter_len):
    blocks, tok_rows, channels = delta_mix.shape
    left_side = delta_mix.reshape(blocks, tok_rows, groups, channels // groups)
    right_side = mixed_ext.reshape(blocks, tok_rows + filter_len, groups, channels // groups)
    products = jnp.einsum("btgc,bsgc->gts", left_side, right_side, precision=highest)
    extent = tok_rows + filter_len
    flipped = products[:, :, ::-1]
    padded = jnp.pad(flipped, ((0, 0), (0, 0), (0, tok_rows)))
    flat_rows = padded.reshape(groups, -1)[:, : tok_rows * (extent + tok_rows - 1)]
    skewed = flat_rows.reshape(groups, tok_rows, extent + tok_rows - 1)
    column_sums = jnp.sum(skewed, axis=1)
    return column_sums[:, tok_rows - 1 : tok_rows - 1 + filter_len]


def local(grad_output, block_input, query_branch, key_branch, value_branch, out_weight, filters):
    filter_len = filters.shape[1]
    groups = filters.shape[0]
    tok_rows = query_branch.shape[1]
    channels = query_branch.shape[2]
    grads_all, inputs_all = (
        lax.all_gather(grad_output[0], "col", axis=0, tiled=True),
        lax.all_gather(block_input[0], "col", axis=0, tiled=True),
    )
    row_devices = lax.axis_size("row")
    sub_width = channels // row_devices
    delta_turned = lax.psum_scatter(
        lax.dot_general(
            out_weight, grads_all, (((0,), (1,)), ((), ())), preferred_element_type=jnp.float32
        ),
        "row",
        scatter_dimension=0,
        tiled=True,
    )
    queries, keys_here, values_here = (
        lax.all_to_all(query_branch[0], "row", split_axis=1, concat_axis=0, tiled=True),
        lax.all_to_all(key_branch[0], "row", split_axis=1, concat_axis=0, tiled=True),
        lax.all_to_all(value_branch[0], "row", split_axis=1, concat_axis=0, tiled=True),
    )
    delta_out = delta_turned.T
    local_groups = sub_width // (channels // groups)
    first_group = lax.axis_index("row") * local_groups
    my_taps = lax.dynamic_slice_in_dim(filters, first_group, local_groups, 0)
    mixed = keys_here.astype(jnp.float32) * values_here.astype(jnp.float32)
    mixed_blocks = mixed.reshape(row_devices, tok_rows, sub_width)
    earlier = jnp.concatenate(
        [
            jnp.zeros((1, filter_len, sub_width), jnp.float32),
            mixed_blocks[:-1, tok_rows - filter_len :],
        ],
        axis=0,
    )
    mixed_ext = jnp.concatenate([earlier, mixed_blocks], axis=1)
    conv_out = grouped_apply(toeplitz(my_taps, tok_rows, True), mixed_ext, local_groups).reshape(
        -1, sub_width
    )
    gated = (queries.astype(jnp.float32) * conv_out).astype(jnp.bfloat16)
    delta_mix = delta_out * queries.astype(jnp.float32)
    delta_blocks = delta_mix.reshape(row_devices, tok_rows, sub_width)
    later_part = jnp.concatenate(
        [delta_blocks[1:, :filter_len], jnp.zeros((1, filter_len, sub_width), jnp.float32)], axis=0
    )
    delta_ext = jnp.concatenate([delta_blocks, later_part], axis=1)
    delta_conv = grouped_apply(toeplitz(my_taps, tok_rows, False), delta_ext, local_groups).reshape(
        -1, sub_width
    )
    delta_value = (delta_conv * keys_here.astype(jnp.float32)).astype(jnp.bfloat16)
    my_terms = taps_partial(delta_blocks, mixed_ext, local_groups, filter_len)
    taps_local = lax.dynamic_update_slice_in_dim(
        jnp.zeros(filters.shape, jnp.float32), my_terms, first_group, 0
    )
    gated_all, value_all = (
        lax.all_gather(gated, "row", axis=1, tiled=True),
        lax.all_gather(delta_value, "row", axis=1, tiled=True),
    )
    out_grad = lax.dot_general(
        grads_all, gated_all, (((0,), (0,)), ((), ())), preferred_element_type=jnp.float32
    )
    value_grad = lax.dot_general(
        value_all, inputs_all, (((0,), (0,)), ((), ())), preferred_element_type=jnp.float32
    )
    out_grad, value_grad = lax.psum((out_grad, value_grad), "dp")
    taps_total = lax.psum(taps_local, ("row", "dp"))
    return (out_grad, value_grad, taps_total)


def solution(mesh):
    in_specs = (
        P("dp", "col", "row"),
        P("dp", "col", "row"),
        P("dp", "row", "col"),
        P("dp", "row", "col"),
        P("dp", "row", "col"),
        P("row", "col"),
        P("col", None),
    )
    out_specs = (P("row", "col"), P("col", "row"), P("col", None))
    return jax.shard_map(local, mesh=mesh, in_specs=in_specs, out_specs=out_specs, check_vma=False)
```

profile of v0, /device:TPU:120, one launch (start us, length us, event | category | flops | bytes accessed | tf_op | source)
XLA Modules:
  0.0 688.4 jit_solution(379694975442089937)
XLA Ops:
  7.2 0.7 all-gather.11.cloned.1.call-update
  8.0 47.9 %all-gather.11.cloned.1.call-done = bf16[1,2048,512]{2,1,0:T(8,128)(2,1)} async-done(((bf16[1,128,512]{2,1,0:T(8,128)(2,1)}), bf16[1,2048,512]{2,1,0:T(8,128)(2,1)}) %all-gather.11.cloned.1.call-update) | async-done | bytes 2097168 | tf_op jit(solution)/shard_map/all_gather | solution.py:46
  55.9 4.8 fusion.2
  60.7 0.9 copy-done.2
  61.6 0.8 copy.40
  62.4 7.5 %all-to-all-start.2 = ((bf16[128,16,32]{0,2,1:T(8,128)(2,1)}), bf16[128,16,32]{0,2,1:T(8,128)(2,1)S(1)}, u32[]{:S(2)}, u32[]{:S(2)}) async-start(bf16[128,16,32]{0,2,1:T(8,128)(2,1)} %bitcast.4), calls=%async_computation.2 | async-start | bytes 262144 | tf_op jit(solution)/shard_map/all_to_all | solution.py:62
  69.9 0.1 fusion.30
  70.0 0.1 copy.66
  70.1 0.7 constant_dynamic-slice_fusion
  70.8 0.8 copy.38
  71.6 0.1 copy.62
  71.7 109.0 %gather_fusion = f32[32768,2]{1,0:T(8,128)} fusion(f32[2,128]{0,1:T(8,128)S(1)} %copy.62, s32[32768]{0:T(1024)S(1)} %broadcast_clamp_fusion.1), kind=kCustom, calls=%fused_computation.clone | custom fusion | bytes 655360 | tf_op jit(solution)/shard_map/jit(_take)/gather | solution.py:15
  180.7 10.0 %copy.46 = f32[128,256,2]{1,0,2:T(8,128)S(1)} copy(f32[128,256,2]{2,1,0:T(8,128)} %bitcast.113) | data formatting | bytes 524288 | tf_op jit(solution)/shard_map/jit(_take)/gather | solution.py:15
  190.7 0.8 copy.36
  191.4 0.2 fusion.35
  191.6 7.5 %all-to-all-start.1 = ((bf16[128,16,32]{0,2,1:T(8,128)(2,1)}), bf16[128,16,32]{0,2,1:T(8,128)(2,1)S(1)}, u32[]{:S(2)}, u32[]{:S(2)}) async-start(bf16[128,16,32]{0,2,1:T(8,128)(2,1)} %bitcast.2), calls=%async_computation.1 | async-start | bytes 262144 | tf_op jit(solution)/shard_map/all_to_all | solution.py:61
  199.2 5.5 all-to-all-done.1
  204.6 6.3 all-to-all-start
  211.1 0.1 slice.19
  211.2 0.1 copy_dynamic-update-slice_fusion
  211.3 0.6 convolution_bitcast_fusion.2
  211.9 0.1 copy.47
  212.0 4.5 all-to-all-done
  216.6 1.7 bitcast_multiply_fusion.2
  218.4 0.5 all-gather.13.cloned.1.call-update
  219.0 0.1 copy.69
  219.1 109.0 %gather_fusion.1 = f32[32768,2]{1,0:T(8,128)} fusion(f32[2,128]{0,1:T(8,128)S(1)} %copy.62, s32[32768]{0:T(1024)S(1)} %broadcast_clamp_fusion), kind=kCustom, calls=%fused_computation.1.clone | custom fusion | bytes 655360 | tf_op jit(solution)/shard_map/jit(_take)/gather | solution.py:15
  328.1 10.1 %copy.51 = f32[128,256,2]{1,0,2:T(8,128)S(1)} copy(f32[128,256,2]{2,1,0:T(8,128)} %bitcast.112) | data formatting | bytes 524288 | tf_op jit(solution)/shard_map/jit(_take)/gather | solution.py:15
  338.2 0.1 fusion.34
  338.3 0.1 slice.21
  338.4 0.1 copy.50
  338.6 0.1 copy.49
  338.7 0.6 convolution_bitcast_fusion.1
  339.3 0.1 copy.52
  339.4 0.7 fusion.13
  340.2 0.0 all-reduce.6.cloned.1.call-start
  340.2 4.5 fusion.6
  344.7 3.9 all-gather.13.cloned.1.call-done
  348.6 87.2 %all-gather.9.cloned.1.call-done = bf16[2048,512]{0,1:T(8,128)(2,1)} async-done(((bf16[2048,32]{0,1:T(8,128)(2,1)}), bf16[2048,512]{0,1:T(8,128)(2,1)}) %all-gather.9.cloned.1.call-update) | async-done | bytes 2097168 | tf_op jit(solution)/shard_map/all_gather | solution.py:98
  435.8 4.4 fusion
  440.3 0.8 convolution_bitcast_fusion
  441.1 0.4 rev.3
  441.5 0.3 copy.71
  441.8 0.6 reshape.76
  442.5 0.1 slice_dynamic-update-slice_fusion
  442.5 235.4 %psum.23 = f32[32,128]{1,0:T(8,128)} all-reduce(f32[32,128]{1,0:T(8,128)S(1)} %slice_dynamic-update-slice_fusion), channel_id=1, replica_groups=mesh['row'=16,'col'=16,'dp'=2] {'row','dp'}, use_global_device_ids=true, to_apply=%region_4.6 | all-reduce | flops 4096 | bytes 32768 | tf_op jit(solution)/shard_map/psum | solution.py:107
  677.9 2.6 copy.54
  680.5 1.0 copy.88
  (39 shorter events, 0.7 us)
Async XLA Ops:
  7.2 48.7 %copy-start = (bf16[512,512]{1,0:T(8,128)(2,1)S(1)}, bf16[512,512]{1,0:T(8,128)(2,1)}, u32[]{:S(2)}) copy-start(bf16[512,512]{1,0:T(8,128)(2,1)} %param.14) | copy-start | bytes 1572868
  7.2 48.7 %all-gather.11.cloned.1.call-start = ((), (), s32[]{:S(2)}) async-start(), calls=%async_computation.7 | async-start | bytes 2228224 | tf_op jit(solution)/shard_map/all_gather | solution.py:46
  7.9 208.7 %reduce-scatter.2.cloned.1.call-start = ((), (), s32[]{:S(2)}) async-start(), calls=%async_computation.5 | async-start | bytes 4456448 | tf_op jit(solution)/shard_map/reduce_scatter | solution.py:51
  60.7 0.9 copy-start.2
  60.7 10.1 %copy-start.3 = (bf16[1,128,512]{2,1,0:T(8,128)(2,1)S(1)}, bf16[1,128,512]{2,1,0:T(8,128)(2,1)}, u32[]{:S(2)}) copy-start(bf16[1,128,512]{2,1,0:T(8,128)(2,1)} %param.12) | copy-start | bytes 393220
  62.4 129.2 %all-to-all-start.2 = ((bf16[128,16,32]{0,2,1:T(8,128)(2,1)}), bf16[128,16,32]{0,2,1:T(8,128)(2,1)S(1)}, u32[]{:S(2)}, u32[]{:S(2)}) async-start(bf16[128,16,32]{0,2,1:T(8,128)(2,1)} %bitcast.4), calls=%async_computation.2 | async-start | bytes 262144 | tf_op jit(solution)/shard_map/all_to_all | solution.py:62
  180.7 10.0 %copy-start.4 = (bf16[1,128,512]{2,1,0:T(8,128)(2,1)S(1)}, bf16[1,128,512]{2,1,0:T(8,128)(2,1)}, u32[]{:S(2)}) copy-start(bf16[1,128,512]{2,1,0:T(8,128)(2,1)} %param.11) | copy-start | bytes 393220
  191.6 13.0 %all-to-all-start.1 = ((bf16[128,16,32]{0,2,1:T(8,128)(2,1)}), bf16[128,16,32]{0,2,1:T(8,128)(2,1)S(1)}, u32[]{:S(2)}, u32[]{:S(2)}) async-start(bf16[128,16,32]{0,2,1:T(8,128)(2,1)} %bitcast.2), calls=%async_computation.1 | async-start | bytes 262144 | tf_op jit(solution)/shard_map/all_to_all | solution.py:61
  204.6 11.9 %all-to-all-start = ((bf16[128,16,32]{0,2,1:T(8,128)(2,1)}), bf16[128,16,32]{0,2,1:T(8,128)(2,1)S(1)}, u32[]{:S(2)}, u32[]{:S(2)}) async-start(bf16[128,16,32]{0,2,1:T(8,128)(2,1)} %bitcast), calls=%async_computation | async-start | bytes 262144 | tf_op jit(solution)/shard_map/all_to_all | solution.py:60
  211.0 129.3 %all-gather.7.cloned.1.call-start = ((), (), s32[]{:S(2)}) async-start(), calls=%async_computation.4 | async-start | bytes 2228224 | tf_op jit(solution)/shard_map/all_gather | solution.py:97
  218.3 130.3 %all-gather.13.cloned.1.call-start = ((), (), s32[]{:S(2)}) async-start(), calls=%async_computation.8 | async-start | bytes 2228224 | tf_op jit(solution)/shard_map/all_gather | solution.py:47
  218.9 216.9 %all-gather.9.cloned.1.call-start = ((), (), s32[]{:S(2)}) async-start(), calls=%async_computation.6 | async-start | bytes 2228224 | tf_op jit(solution)/shard_map/all_gather | solution.py:98
  340.2 337.8 %all-reduce.6.cloned.1.call-start = ((), (), s32[]{:S(2)}) async-start(), calls=%async_computation.9 | async-start | bytes 4194304 | tf_op jit(solution)/shard_map/psum | solution.py:106
  677.9 2.6 copy-start.1
Sparse Core Ops, SparseCore 0:
  10.1 45.6 all-gather.10
  60.8 102.5 reduce-scatter.1
  218.4 82.8 all-gather.6
  303.3 45.2 all-gather.12
  351.1 84.6 all-gather.8
  440.4 125.1 all-reduce.5
where the time goes:
time: 690 us; the launch traced here: 688 us
  local copies, waits for them, and re-layouts  248 us (36%)
  blocking collectives  235 us (34%)
  waiting for transfers between devices  150 us (22%)
  starting transfers between devices  21.6 us (3%)
  matrix products  15.8 us (2%)
  between operations  14.4 us (2%)
    gather x4, local copies, waits for them, and re-layouts, toeplitz(): picked = jnp.take(taps, jnp.clip(lagged, 0, filter_len - 1), axis=1)  238 us
    psum x1, blocking collectives, local(): taps_total = lax.psum(taps_local, ('row', 'dp'))  235 us
    all_gather x1, waiting for transfers between devices, local(): lax.all_gather(delta_value, 'row', axis=1, tiled=True)  87.2 us
    all_gather x1, waiting for transfers between devices, local(): lax.all_gather(grad_output[0], 'col', axis=0, tiled=True)  47.9 us
  transfers between devices with their start and end apart: 9, of which 5 were waited for; matrix products, arithmetic and copies ran while one was open for 36% of the time, Pallas kernels for 0%

commit v1 on v0

v1 whole, which is shorter than its diff:
```python
import jax
import jax.numpy as jnp
from jax import lax
from jax.experimental import pallas as pl
from jax.experimental.pallas import tpu as pltpu
from jax.sharding import PartitionSpec as P

MESH = pl.DeviceIdType.MESH
F32 = jnp.float32
BF16 = jnp.bfloat16
NX, NYL, NY, NZ = 4, 4, 8, 8
BLK = 16
TOK = 128
SUB = 32
H0 = 9
SEMS = 94


def exact_dot(a, b, dims):
    return lax.dot_general(a, b, (dims, ((), ())), precision=lax.Precision.HIGHEST, preferred_element_type=F32)


def skew(rows, left):
    which = lax.broadcasted_iota(jnp.int32, rows.shape, 0)
    n = rows.shape[1]
    for bit in range(7):
        step = n - (1 << bit) if left else 1 << bit
        rows = jnp.where(((which >> bit) & 1) == 1, pltpu.roll(rows, step, 1), rows)
    return rows


def kernel(
    g_hbm, i_hbm, q_ref, k_ref, v_ref, w_ref, f_ref,
    out_ref, val_ref, tap_ref,
    xa, wt, t3, qkv, gat, dlv, part, r1, r2, ry, acc, fown, fall,
    loc_sem, a2a_send, a2a_recv, tap_send, tap_recv, send_sem, recv_sem,
):
    row, col, dp = lax.axis_index("row"), lax.axis_index("col"), lax.axis_index("dp")
    X, YL, Z, K = lax.div(row, NYL), lax.rem(row, NYL), lax.div(col, 2), lax.rem(col, 2)
    Y = dp * NYL + YL

    def at(x, y, z, k):
        return {"row": x * NYL + lax.rem(y, NYL), "col": z * 2 + k, "dp": lax.div(y, NYL)}

    def wx(d):
        return lax.rem(X + (d + NX), NX)

    def wy(d):
        return lax.rem(Y + (d + NY), NY)

    def wz(d):
        return lax.rem(Z + (d + NZ), NZ)

    xp, xm = at(wx(1), Y, Z, K), at(wx(-1), Y, Z, K)
    yp, ym = at(X, wy(1), Z, K), at(X, wy(-1), Z, K)
    zp, zm = at(X, Y, wz(1), K), at(X, Y, wz(-1), K)
    mate = at(X, Y, Z, 1 - K)
    twin = at(X, wy(4), Z, K)

    copies = []

    def send(src, dst, to):
        n = len(copies)
        c = pltpu.make_async_remote_copy(src, dst, send_sem.at[n], recv_sem.at[n], device_id=to, device_id_type=MESH)
        c.start()
        copies.append(c)
        return c

    own_g = pltpu.make_async_copy(g_hbm.at[0], xa.at[0, col], loc_sem.at[0])
    own_i = pltpu.make_async_copy(i_hbm.at[0], xa.at[2, col], loc_sem.at[1])
    own_g.start()
    own_i.start()

    barrier = pltpu.get_barrier_semaphore()
    me = row * 2 + dp

    def group_peer(s):
        other = lax.rem(me + s, 32)
        return {"row": lax.div(other, 2), "col": col, "dp": lax.rem(other, 2)}

    @pl.loop(1, 32)
    def _(s):
        pl.semaphore_signal(barrier, inc=1, device_id=group_peer(s), device_id_type=MESH)

    for other in (zp, zm, mate):
        pl.semaphore_signal(barrier, inc=1, device_id=other, device_id_type=MESH)

    for n, ref in enumerate((q_ref, k_ref, v_ref)):
        t3[:, n] = ref[0].astype(F32).T.astype(BF16).reshape(BLK, SUB, TOK)
    own_g.wait()
    own_i.wait()
    pl.semaphore_wait(barrier, 34)

    def ring_z(lo, n):
        def s(z):
            return xa.at[pl.ds(lo, n), z * 2 + K]

        def half(z, h):
            return xa.at[pl.ds(lo, n), z * 2 + K, pl.ds(h * 64, 64)]

        mates = []
        ups, downs = [], []
        for step in range(3):
            up, down = s(wz(-step)), s(wz(step))
            ups.append(send(up, up, zp))
            downs.append(send(down, down, zm))
            if step == 0:
                mates.append(send(s(Z), s(Z), mate))
            else:
                mates.append(send(up, up, mate))
                mates.append(send(down, down, mate))
            yield
            ups[-1].wait_recv()
            downs[-1].wait_recv()
        up, down = half(wz(-3), 0), half(wz(3), 1)
        ups.append(send(up, up, zp))
        downs.append(send(down, down, zm))
        for z in (wz(-3), wz(3)):
            mates.append(send(s(z), s(z), mate))
        yield
        ups[-1].wait_recv()
        downs[-1].wait_recv()
        far = s(wz(4))
        mates.append(send(far, far, mate))
        yield
        for c in mates:
            c.wait_recv()

    def gather_xy(buf):
        n1 = BLK - H0

        def c0(y, lo=0, n=H0):
            return buf.at[X, y, pl.ds(lo, n)]

        def c1(x, lo=0, n=n1):
            return buf.at[x, Y, pl.ds(H0 + lo, n)]

        def rows_of(y, lo=0, n=NX):
            return buf.at[pl.ds(lo, n), y, pl.ds(H0, n1)]

        def cols_of(x, lo=0, n=NY):
            return buf.at[x, pl.ds(lo, n), pl.ds(0, H0)]

        def both(up, down, to_up, to_down):
            return send(up, up, to_up), send(down, down, to_down)

        def arrived(pair):
            pair[0].wait_recv()
            pair[1].wait_recv()

        ha, hb = H0 // 2, n1 // 2
        a = both(c0(Y), c0(Y), yp, ym)
        b = both(c1(X), c1(X), xp, xm)
        yield
        arrived(b)
        b = both(c1(wx(-1), 0, hb), c1(wx(1), hb, n1 - hb), xp, xm)
        yield
        arrived(a)
        a = both(c0(wy(-1)), c0(wy(1)), yp, ym)
        yield
        arrived(b)
        b = both(rows_of(Y), rows_of(Y), yp, ym)
        yield
        arrived(a)
        a = both(c0(wy(-2)), c0(wy(2)), yp, ym)
        yield
        arrived(a)
        a = both(c0(wy(-3), 0, ha), c0(wy(3), ha, H0 - ha), yp, ym)
        yield
        arrived(a)
        a = both(cols_of(X), cols_of(X), xp, xm)
        yield
        arrived(b)
        b = both(rows_of(wy(-1)), rows_of(wy(1)), yp, ym)
        yield
        arrived(a)
        a = both(cols_of(wx(-1), 0, 4), cols_of(wx(1), 4, 4), xp, xm)
        yield
        arrived(b)
        b = both(rows_of(wy(-2)), rows_of(wy(2)), yp, ym)
        yield
        arrived(b)
        b = both(rows_of(wy(-3), 0, 2), rows_of(wy(3), 2, 2), yp, ym)
        yield
        arrived(a)
        arrived(b)

    z1 = ring_z(0, 1)
    next(z1)
    tw_g = send(xa.at[0, col], xa.at[1, col], twin)
    tw_i = send(xa.at[2, col], xa.at[3, col], twin)

    qkv[row] = t3[row]

    @pl.loop(1, 16)
    def _(s):
        other = lax.rem(row + s, 16)
        pltpu.make_async_remote_copy(
            t3.at[other], qkv.at[row], a2a_send, a2a_recv,
            device_id={"row": other, "col": col, "dp": dp}, device_id_type=MESH,
        ).start()

    wt[...] = w_ref[...].astype(F32).T.astype(BF16)
    next(z1)

    at_s = lax.broadcasted_iota(jnp.int32, (TOK, TOK), 0)
    at_t = lax.broadcasted_iota(jnp.int32, (TOK, TOK), 1)
    same = at_t >= at_s
    tables = []
    for grp in range(2):
        taps = jnp.broadcast_to(f_ref[pl.ds(row * 2 + grp, 1), :], (TOK, TOK))
        wrapped = skew(taps, False)
        tables.append((jnp.where(same, wrapped, 0.0), jnp.where(same, 0.0, wrapped)))

    next(z1)
    pltpu.make_async_copy(qkv.at[pl.ds(0, 15)], qkv.at[pl.ds(0, 15)], a2a_recv).wait()

    def signal_rows(n, grp):
        return qkv[:, n, pl.ds(16 * grp, 16), :].astype(F32).reshape(BLK * 16, TOK)

    zeros16 = jnp.zeros((16, TOK), F32)
    mixes = []
    for grp in range(2):
        table, before = tables[grp]
        mixed = signal_rows(1, grp) * signal_rows(2, grp)
        earlier = jnp.concatenate([zeros16, mixed[:-16]], axis=0)
        mixes.append((mixed, earlier))
        conv = exact_dot(mixed, table, ((1,), (0,))) + exact_dot(earlier, before, ((1,), (0,)))
        gated = (signal_rows(0, grp) * conv).astype(BF16)
        gat[X, Y, :, pl.ds(16 * grp, 16), :] = gated.reshape(BLK, 16, TOK)
    next(z1)
    ag = gather_xy(gat)
    next(ag)
    next(z1)
    tw_g.wait_recv()
    tw_i.wait_recv()
    z2 = ring_z(1, 3)
    next(z2)
    next(z1, None)

    def product(j):
        left = wt[pl.ds(pl.multiple_of(wx(j) * 128, 128), 128), :]

        @pl.loop(0, 8)
        def _(bp):
            right = xa[0, pl.ds(bp * 2, 2)].reshape(2 * TOK, 512)
            res = lax.dot_general(left, right, (((1,), (1,)), ((), ())), preferred_element_type=F32)
            half, at_blk = lax.div(bp, 4), lax.rem(bp, 4) * 2
            for n in range(2):
                part[j, half, :, at_blk + n] = res[:, n * TOK : (n + 1) * TOK].reshape(NYL, SUB, TOK)

    product(2)
    far_a = send(part.at[2, 0], r1.at[0], xp)
    far_b = send(part.at[2, 1], r1.at[1], xm)
    product(1)
    near_a = send(part.at[1, 1], r2.at[0, 1], xp)
    product(3)
    near_b = send(part.at[3, 0], r2.at[1, 0], xm)
    product(0)
    next(ag)
    next(ag)
    next(ag)
    next(z2)
    far_a.wait_recv()
    part[1, 0] = part[1, 0] + r1[0]
    late_a = send(part.at[1, 0], r2.at[0, 0], xp)
    far_b.wait_recv()
    part[3, 1] = part[3, 1] + r1[1]
    late_b = send(part.at[3, 1], r2.at[1, 1], xm)
    next(ag)
    next(ag)
    next(z2)
    next(ag)
    for c in (near_a, near_b, late_a, late_b):
        c.wait_recv()
    cross = []
    for half in range(2):
        part[0, half] = part[0, half] + (r2[0, half] + r2[1, half])
        for d in range(1, 4):
            peer = lax.rem(YL + d, NYL)
            cross.append(send(part.at[0, half, peer], ry.at[half, d - 1], at(X, dp * NYL + peer, Z, K)))
    next(ag)
    next(z2)
    next(ag)
    for c in cross:
        c.wait_recv()
    summed = []
    for half in range(2):
        summed.append(part[0, half, YL] + ((ry[half, 0] + ry[half, 1]) + ry[half, 2]))
    delta = jnp.concatenate(summed, axis=0)

    tap_rows = []
    for grp in range(2):
        table, before = tables[grp]
        mixed, earlier = mixes[grp]
        delta_mix = delta[:, 16 * grp : 16 * grp + 16].reshape(BLK * 16, TOK) * signal_rows(0, grp)
        later = jnp.concatenate([delta_mix[16:], zeros16], axis=0)
        conv = exact_dot(delta_mix, table, ((1,), (1,))) + exact_dot(later, before, ((1,), (1,)))
        dlv[X, Y, :, pl.ds(16 * grp, 16), :] = (conv * signal_rows(1, grp)).astype(BF16).reshape(BLK, 16, TOK)
        tap_rows.append((delta_mix, mixed, earlier))
    ag2 = gather_xy(dlv)
    next(ag2)
    fown[...] = jnp.zeros_like(fown)
    for grp in range(2):
        delta_mix, mixed, earlier = tap_rows[grp]
        here = exact_dot(mixed.T, delta_mix, ((1,), (0,)))
        there = exact_dot(earlier.T, delta_mix, ((1,), (0,)))
        lags = skew(jnp.where(same, here, there), True)
        fown[pl.ds(grp, 1), :] = jnp.sum(lags, axis=0, keepdims=True)
    mine = dp * 16 + row
    fall[mine] = fown[...]

    @pl.loop(1, 32)
    def _(s):
        pltpu.make_async_remote_copy(
            fown, fall.at[mine], tap_send, tap_recv, device_id=group_peer(s), device_id_type=MESH
        ).start()

    next(ag2)
    next(ag)
    next(ag2)
    next(ag2)
    next(z2)
    next(ag)
    next(ag2)
    next(ag2)
    next(ag, None)
    next(ag2)
    next(z2, None)

    def outer(buf, arr, total):
        total[...] = jnp.zeros_like(total)
        for d in range(2):
            rel = lax.rem(dp + d, 2)

            @pl.loop(0, 4)
            def _(step):
                left = jnp.concatenate(
                    [buf[:, pl.ds(d * NYL, NYL), step * 4 + n].reshape(512, TOK) for n in range(4)], axis=1
                )
                right = xa[arr * 2 + rel, pl.ds(step * 4, 4)].reshape(512, 512)
                total[...] += jnp.dot(left, right, preferred_element_type=F32)

    outer(gat, 0, acc)
    next(ag2)
    out_ref[...] = acc[...].T
    for _ in ag2:
        pass
    outer(dlv, 1, val_ref)

    pltpu.make_async_copy(fall.at[pl.ds(0, 31)], fall.at[pl.ds(0, 31)], tap_recv).wait()
    for r in range(16):
        tap_ref[pl.ds(2 * r, 2), :] = fall[r, 0:2, :] + fall[16 + r, 0:2, :]

    pltpu.make_async_copy(t3.at[pl.ds(0, 15)], t3.at[pl.ds(0, 15)], a2a_send).wait()
    pltpu.make_async_copy(fall.at[pl.ds(0, 31)], fall.at[pl.ds(0, 31)], tap_send).wait()
    for c in copies:
        c.wait_send()


def local(grad_output, block_input, query_branch, key_branch, value_branch, out_weight, filters):
    vmem = pl.BlockSpec(memory_space=pltpu.VMEM)
    hbm = pl.BlockSpec(memory_space=pl.ANY)
    return pl.pallas_call(
        kernel,
        out_shape=(
            jax.ShapeDtypeStruct((512, 512), F32),
            jax.ShapeDtypeStruct((512, 512), F32),
            jax.ShapeDtypeStruct((32, 128), F32),
        ),
        in_specs=[hbm, hbm, vmem, vmem, vmem, vmem, vmem],
        out_specs=(vmem, vmem, vmem),
        scratch_shapes=[
            pltpu.VMEM((4, BLK, TOK, 512), BF16),
            pltpu.VMEM((512, 512), BF16),
            pltpu.VMEM((BLK, 3, SUB, TOK), BF16),
            pltpu.VMEM((BLK, 3, SUB, TOK), BF16),
            pltpu.VMEM((NX, NY, BLK, SUB, TOK), BF16),
            pltpu.VMEM((NX, NY, BLK, SUB, TOK), BF16),
            pltpu.VMEM((NX, 2, NYL, 8, SUB, TOK), F32),
            pltpu.VMEM((2, NYL, 8, SUB, TOK), F32),
            pltpu.VMEM((2, 2, NYL, 8, SUB, TOK), F32),
            pltpu.VMEM((2, 3, 8, SUB, TOK), F32),
            pltpu.VMEM((512, 512), F32),
            pltpu.VMEM((8, 128), F32),
            pltpu.VMEM((32, 8, 128), F32),
            pltpu.SemaphoreType.DMA((2,)),
            pltpu.SemaphoreType.DMA,
            pltpu.SemaphoreType.DMA,
            pltpu.SemaphoreType.DMA,
            pltpu.SemaphoreType.DMA,
            pltpu.SemaphoreType.DMA((SEMS,)),
            pltpu.SemaphoreType.DMA((SEMS,)),
        ],
        compiler_params=pltpu.CompilerParams(collective_id=0, has_side_effects=True, vmem_limit_bytes=60 * 1024 * 1024),
    )(grad_output, block_input, query_branch, key_branch, value_branch, out_weight, filters)


def solution(mesh):
    in_specs = (
        P("dp", "col", "row"),
        P("dp", "col", "row"),
        P("dp", "row", "col"),
        P("dp", "row", "col"),
        P("dp", "row", "col"),
        P("row", "col"),
        P("col", None),
    )
    out_specs = (P("row", "col"), P("col", "row"), P("col", None))
    return jax.shard_map(local, mesh=mesh, in_specs=in_specs, out_specs=out_specs, check_vma=False)
```

time: 690 us -> 173 us (0.25)
  the two profiles are of different devices: /device:TPU:120 before, /device:TPU:8 now
where the time goes in v1:
time: 173 us
  Pallas kernels  169 us (98%)
  local copies, waits for them, and re-layouts  3.93 us (2%)
    pallas_call x1, Pallas kernels, local(): pl.pallas_call(kernel, out_shape=(jax.ShapeDtypeStruct((512, 512), F32),...  169 us
    unnamed x7, local copies, waits for them, and re-layouts  3.93 us

profile of v1, /device:TPU:8, one launch (start us, length us, event | category | flops | bytes accessed | tf_op | source)
XLA Modules:
  0.0 173.1 jit_solution(15990498040518030431)
XLA Ops:
  0.6 168.6 %shard_map.94 = (f32[512,512]{1,0:T(8,128)}, f32[512,512]{1,0:T(8,128)}, f32[32,128]{1,0:T(8,128)}) custom-call(bf16[1,128,512]{2,1,0:T(8,128)(2,1)} %g_hbm.1, bf16[1,128,512]{2,1,0:T(8,128)(2,1)} %i_hbm.1, bf16[1,128,512]{2,1,0:T(8,128)(2,1)} %q_ref.1, bf16[1,128,512]{2,1,0:T(8,128)(2,1)} %k_ref.1, bf16[1,128,512]{2,1,0:T(8,128)(2,1)} %v_ref.1, ...), custom_call_target="tpu_custom_call" | custom-call | tf_op jit(solution)/shard_map/pallas_call | solution.py:364
  169.2 0.0 copy-start
  169.2 2.4 %copy.13 = f32[512,512]{1,0:T(8,128)} copy(f32[512,512]{1,0:T(8,128)} %get-tuple-element.6) | data formatting | bytes 2097152
  171.6 0.0 copy-done
  171.6 0.0 copy-start.1
  171.6 1.0 copy.14
  172.5 0.0 copy-done.1
  172.5 0.6 copy.15
Async XLA Ops:
  169.2 2.4 %copy-start = (f32[512,512]{1,0:T(8,128)S(1)}, f32[512,512]{1,0:T(8,128)}, u32[]{:S(2)}) copy-start(f32[512,512]{1,0:T(8,128)} %get-tuple-element.7) | copy-start | bytes 3145732
  171.6 1.0 copy-start.1

commit v2 on v1

v2 whole, which is shorter than its diff:
```python
import jax
import jax.numpy as jnp
from jax import lax
from jax.experimental import pallas as pl
from jax.experimental.pallas import tpu as pltpu
from jax.sharding import PartitionSpec as P

MESH = pl.DeviceIdType.MESH
F32 = jnp.float32
BF16 = jnp.bfloat16
NX, NYL, NY, NZ = 4, 4, 8, 8
BLK = 16
TOK = 128
SUB = 32
SEMS = 220
AG1 = (10, ((10, 3), (13, 3)))
AG2 = (9, ((9, 4), (13, 3)))
SCHEDULE1 = (
    ("cross", 1), ("late", 3), ("cross", 2), ("cross", 3), ("h0", 1), ("h1", 1), ("h0", 1),
    ("finish", 0), ("finish", 1), ("finish", 2), ("z2", 1), ("finish", 3),
)
SCHEDULE2 = (
    ("g1", 1), ("g0", 1), ("h0", 1), ("h1", 1), ("g0", 1), ("g1", 1), ("h0", 2), ("z2", 1), ("g0", 1), ("h1", 2), ("z2", 1), ("g0", 1), ("g1", 2), ("h0", 1), ("h1", 2), ("taps", 0),
    ("z2", 1), ("g0", 2), ("z2", 1), ("g1", 2), ("h1", 9), ("g0", 2), ("h0", 9), ("z2", 99), ("outer", 0), ("g1", 2), ("g0", 99), ("g1", 99),
)
RDT = BF16


def exact_dot(a, b, dims):
    return lax.dot_general(a, b, (dims, ((), ())), precision=lax.Precision.HIGHEST, preferred_element_type=F32)


def skew(rows, left):
    which = lax.broadcasted_iota(jnp.int32, rows.shape, 0)
    n = rows.shape[1]
    for bit in range(7):
        step = n - (1 << bit) if left else 1 << bit
        rows = jnp.where(((which >> bit) & 1) == 1, pltpu.roll(rows, step, 1), rows)
    return rows


def kernel(
    g_hbm, i_hbm, q_hbm, k_hbm, v_hbm, w_hbm, f_hbm,
    out_ref, val_ref, tap_ref,
    xa, tok, w_ref, f_ref, wt, t3, qkv, gat, dlv, far_out, near_out, late_out, own_sum, r1, r2n, r2l, ry, dsum, acc, fown, fboth, fall,
    loc_sem, a2a_send, a2a_recv, tap_send, tap_recv, send_sem, recv_sem,
):
    row, col, dp = lax.axis_index("row"), lax.axis_index("col"), lax.axis_index("dp")
    X, YL, Z, K = lax.div(row, NYL), lax.rem(row, NYL), lax.div(col, 2), lax.rem(col, 2)
    Y = dp * NYL + YL

    def at(x, y, z, k):
        return {"row": x * NYL + lax.rem(y, NYL), "col": z * 2 + k, "dp": lax.div(y, NYL)}

    def wx(d):
        return lax.rem(X + (d + NX), NX)

    def wy(d):
        return lax.rem(Y + (d + NY), NY)

    def wz(d):
        return lax.rem(Z + (d + NZ), NZ)

    xp, xm = at(wx(1), Y, Z, K), at(wx(-1), Y, Z, K)
    yp, ym = at(X, wy(1), Z, K), at(X, wy(-1), Z, K)
    zp, zm = at(X, Y, wz(1), K), at(X, Y, wz(-1), K)
    mate = at(X, Y, Z, 1 - K)
    twin = at(X, wy(4), Z, K)

    copies = []

    def send(src, dst, to):
        n = len(copies)
        c = pltpu.make_async_remote_copy(src, dst, send_sem.at[n], recv_sem.at[n], device_id=to, device_id_type=MESH)
        c.start()
        copies.append(c)
        return c

    def both(up, down, to_up, to_down):
        return send(up, up, to_up), send(down, down, to_down)

    def arrived(*some):
        for c in some:
            c.wait_recv()

    def run(stream, steps):
        for _ in range(steps):
            next(stream, None)

    own = [
        pltpu.make_async_copy(src, dst, loc_sem.at[n])
        for n, (src, dst) in enumerate((
            (g_hbm.at[0], xa.at[0, col]), (q_hbm.at[0], tok.at[0]), (k_hbm.at[0], tok.at[1]), (v_hbm.at[0], tok.at[2]),
            (i_hbm.at[0], xa.at[2, col]), (w_hbm, w_ref), (f_hbm, f_ref),
        ))
    ]
    for c in own:
        c.start()

    barrier = pltpu.get_barrier_semaphore()
    me = row * 2 + dp

    def group_peer(s):
        other = lax.rem(me + s, 32)
        return {"row": lax.div(other, 2), "col": col, "dp": lax.rem(other, 2)}

    @pl.loop(1, 32)
    def _(s):
        pl.semaphore_signal(barrier, inc=1, device_id=group_peer(s), device_id_type=MESH)

    for other in (zp, zm, mate):
        pl.semaphore_signal(barrier, inc=1, device_id=other, device_id_type=MESH)

    at_s = lax.broadcasted_iota(jnp.int32, (TOK, TOK), 0)
    at_t = lax.broadcasted_iota(jnp.int32, (TOK, TOK), 1)
    same = at_t >= at_s
    for c in own:
        c.wait()
    for n in range(3):
        t3[:, n] = tok[n].astype(F32).T.astype(BF16).reshape(BLK, SUB, TOK)
    qkv[row] = t3[row]
    wt[...] = w_ref[...].astype(F32).T.astype(BF16)
    tables = []
    for grp in range(2):
        taps = jnp.broadcast_to(f_ref[pl.ds(row * 2 + grp, 1), :], (TOK, TOK))
        wrapped = skew(taps, False)
        tables.append((jnp.where(same, wrapped, 0.0), jnp.where(same, 0.0, wrapped)))
    pl.semaphore_wait(barrier, 34)

    mates = {}

    def gather_first():
        def s(z, r):
            return xa.at[0, z * 2 + K, pl.ds(r * 64, 64)]

        def hand(*offsets):
            for o in offsets:
                block = xa.at[0, wz(o) * 2 + K]
                mates[o] = send(block, block, mate)

        pairs = [both(s(Z, r), s(Z, r), zp, zm) for r in range(2)]
        hand(0)
        yield
        for d in (1, 2):
            for r in range(2):
                arrived(*pairs[r])
                pairs[r] = both(s(wz(-d), r), s(wz(d), r), zp, zm)
            hand(-d, d)
            yield
        arrived(*pairs[0])
        up = send(s(wz(-3), 0), s(wz(-3), 0), zp)
        arrived(*pairs[1])
        down = send(s(wz(3), 1), s(wz(3), 1), zm)
        hand(-3, 3)
        yield
        arrived(up, down)
        hand(4)

    def ring_z(lo, n):
        def s(z, first=0, count=TOK):
            return xa.at[pl.ds(lo, n), z * 2 + K, pl.ds(first, count)]

        handed = []
        for step in range(3):
            up, down = s(wz(-step)), s(wz(step))
            pair = both(up, down, zp, zm)
            handed.append(send(up, up, mate))
            if step > 0:
                handed.append(send(down, down, mate))
            yield
            arrived(*pair)
        pair = both(s(wz(-3), 0, 64), s(wz(3), 64, 64), zp, zm)
        for z in (wz(-3), wz(3)):
            handed.append(send(s(z), s(z), mate))
        yield
        arrived(*pair)
        far = s(wz(4))
        handed.append(send(far, far, mate))
        yield
        arrived(*handed)

    def y_first(buf, n0, eager):
        def one(x, o, lo=0, n=n0):
            return buf.at[x, wy(o), pl.ds(lo, n)]

        def cols_of(x, lo=0, n=NY):
            return buf.at[x, pl.ds(lo, n), pl.ds(0, n0)]

        across = {}
        second = []

        def spread(*offsets):
            if eager:
                for o in offsets:
                    across[o] = both(one(X, o), one(X, o), xp, xm)

        def relay(*offsets):
            for o in offsets:
                arrived(*across[o])
                if o in (-1, 0, 2, 4):
                    second.append(send(one(wx(-1), o), one(wx(-1), o), xp))
                else:
                    second.append(send(one(wx(1), o), one(wx(1), o), xm))

        h = n0 // 2
        a = both(one(X, 0), one(X, 0), yp, ym)
        spread(0)
        yield
        for o in (1, 2):
            arrived(*a)
            a = both(one(X, -o), one(X, o), yp, ym)
            spread(-o, o)
            yield
            if eager:
                relay(*((0,) if o == 1 else (-1, 1)))
                yield
        arrived(*a)
        a = both(one(X, -3, 0, h), one(X, 3, h, n0 - h), yp, ym)
        spread(-3, 3)
        yield
        if eager:
            relay(-2, 2)
            yield
        arrived(*a)
        spread(4)
        if eager:
            yield
            relay(-3, 3)
            yield
            relay(4)
            yield
            arrived(*second)
        else:
            yield
            a = both(cols_of(X), cols_of(X), xp, xm)
            yield
            arrived(*a)
            a = both(cols_of(wx(-1), 0, 4), cols_of(wx(1), 4, 4), xp, xm)
            yield
            arrived(*a)

    def x_first(buf, n0, subs):
        n1 = BLK - n0
        h = n1 // 2

        def one(x, lo=0, n=n1):
            return buf.at[x, Y, pl.ds(n0 + lo, n)]

        def rows_of(o, sub, lo=0, n=NX):
            first, count = subs[sub]
            return buf.at[pl.ds(lo, n), wy(o), pl.ds(first, count)]

        b = both(one(X), one(X), xp, xm)
        yield
        arrived(*b)
        b = both(one(wx(-1), 0, h), one(wx(1), h, n1 - h), xp, xm)
        yield
        arrived(*b)
        rings = [both(rows_of(0, n), rows_of(0, n), yp, ym) for n in range(len(subs))]
        yield
        for o in (1, 2, 3):
            for n in range(len(subs)):
                arrived(*rings[n])
                if o < 3:
                    rings[n] = both(rows_of(-o, n), rows_of(o, n), yp, ym)
                else:
                    rings[n] = both(rows_of(-3, n, 0, 2), rows_of(3, n, 2, 2), yp, ym)
                yield
        for n in range(len(subs)):
            arrived(*rings[n])

    offsets = ((0, -1, -2, -3), (1, 2, 3, 4))
    far = [None] * 4
    near = [None] * 4
    late = [None] * 4
    cross = {}

    def product(j, half, p, out):
        left = wt[pl.ds(pl.multiple_of(wx(j) * 128, 128), 128), :]
        right = xa[0, pl.ds(wz(offsets[half][p]) * 2, 2)].reshape(2 * TOK, 512)
        res = lax.dot_general(left, right, (((1,), (1,)), ((), ())), preferred_element_type=F32)
        for n in range(2):
            out[half, p, :, n] = res[:, n * TOK : (n + 1) * TOK].reshape(NYL, SUB, TOK).astype(out.dtype)

    def start_piece(p):
        arrived(mates[offsets[0][p]], mates[offsets[1][p]])
        product(2, 0, p, far_out)
        product(2, 1, p, far_out)
        far[p] = (send(far_out.at[0, p], r1.at[0, p], xp), send(far_out.at[1, p], r1.at[1, p], xm))
        product(1, 1, p, near_out)
        product(3, 0, p, near_out)
        near[p] = (send(near_out.at[1, p], r2n.at[1, p], xp), send(near_out.at[0, p], r2n.at[0, p], xm))
        product(1, 0, p, late_out)
        product(3, 1, p, late_out)
        product(0, 0, p, own_sum)
        product(0, 1, p, own_sum)

    def start_late(p):
        sent = []
        for half, to in ((0, xp), (1, xm)):
            arrived(far[p][half])
            late_out[half, p] = late_out[half, p] + r1[half, p].astype(F32)
            sent.append(send(late_out.at[half, p], r2l.at[half, p], to))
        late[p] = sent

    def start_cross(p):
        arrived(*near[p], *late[p])
        for half in range(2):
            own_sum[half, p] = own_sum[half, p] + (r2n[half, p].astype(F32) + r2l[half, p])
            for d in range(1, 4):
                peer = lax.rem(YL + d, NYL)
                cross[half, p, d] = send(own_sum.at[half, p, peer], ry.at[half, p, d - 1], at(X, dp * NYL + peer, Z, K))

    def finish(p):
        for half in range(2):
            arrived(*[cross[half, p, d] for d in range(1, 4)])
            total = own_sum[half, p, YL] + ((ry[half, p, 0] + ry[half, p, 1]) + ry[half, p, 2])
            dsum[pl.ds(wz(offsets[half][p]) * 2, 2)] = total

    z1 = gather_first()
    run(z1, 1)

    @pl.loop(1, 16)
    def _(s):
        other = lax.rem(row + s, 16)
        pltpu.make_async_remote_copy(
            t3.at[other], qkv.at[row], a2a_send, a2a_recv,
            device_id={"row": other, "col": col, "dp": dp}, device_id_type=MESH,
        ).start()

    tw_g = send(xa.at[0, col], xa.at[1, col], twin)
    tw_i = send(xa.at[2, col], xa.at[3, col], twin)
    run(z1, 1)
    start_piece(0)
    run(z1, 1)
    start_piece(1)
    start_late(0)
    run(z1, 1)
    start_piece(2)
    start_late(1)
    pltpu.make_async_copy(qkv.at[pl.ds(0, 15)], qkv.at[pl.ds(0, 15)], a2a_recv).wait()

    def signal_rows(n, grp):
        return qkv[:, n, pl.ds(16 * grp, 16), :].astype(F32).reshape(BLK * 16, TOK)

    zeros16 = jnp.zeros((16, TOK), F32)
    mixes = []
    for grp in range(2):
        table, before = tables[grp]
        mixed = signal_rows(1, grp) * signal_rows(2, grp)
        earlier = jnp.concatenate([zeros16, mixed[:-16]], axis=0)
        mixes.append((mixed, earlier))
        conv = exact_dot(mixed, table, ((1,), (0,))) + exact_dot(earlier, before, ((1,), (0,)))
        gated = (signal_rows(0, grp) * conv).astype(BF16)
        gat[X, Y, :, pl.ds(16 * grp, 16), :] = gated.reshape(BLK, 16, TOK)
    h0 = y_first(gat, AG1[0], False)
    h1 = x_first(gat, *AG1)
    run(h1, 1)
    run(h0, 1)
    start_cross(0)
    run(z1, 1)
    start_piece(3)
    start_late(2)

    def ring_rest():
        arrived(tw_g, tw_i)
        yield from ring_z(1, 3)

    z2 = ring_rest()
    for stream, steps in SCHEDULE1:
        if stream in ("late", "cross", "finish"):
            {"late": start_late, "cross": start_cross, "finish": finish}[stream](steps)
        else:
            run({"h0": h0, "h1": h1, "z2": z2}[stream], steps)
    delta = dsum[...]

    tap_rows = []
    for grp in range(2):
        table, before = tables[grp]
        mixed, earlier = mixes[grp]
        delta_mix = delta[:, 16 * grp : 16 * grp + 16].reshape(BLK * 16, TOK) * signal_rows(0, grp)
        later = jnp.concatenate([delta_mix[16:], zeros16], axis=0)
        conv = exact_dot(delta_mix, table, ((1,), (1,))) + exact_dot(later, before, ((1,), (1,)))
        dlv[X, Y, :, pl.ds(16 * grp, 16), :] = (conv * signal_rows(1, grp)).astype(BF16).reshape(BLK, 16, TOK)
        tap_rows.append((delta_mix, mixed, earlier))
    g0 = y_first(dlv, AG2[0], True)
    g1 = x_first(dlv, *AG2)
    run(g1, 1)
    run(g0, 1)
    fown[...] = jnp.zeros_like(fown)
    for grp in range(2):
        delta_mix, mixed, earlier = tap_rows[grp]
        here = exact_dot(mixed.T, delta_mix, ((1,), (0,)))
        there = exact_dot(earlier.T, delta_mix, ((1,), (0,)))
        lags = skew(jnp.where(same, here, there), True)
        fown[pl.ds(grp, 1), :] = jnp.sum(lags, axis=0, keepdims=True)
    tap_twin = send(fown, fboth, twin)

    def outer(buf, arr, total):
        total[...] = jnp.zeros_like(total)
        for d in range(2):
            rel = lax.rem(dp + d, 2)

            @pl.loop(0, 4)
            def _(step):
                left = jnp.concatenate(
                    [buf[:, pl.ds(d * NYL, NYL), step * 4 + n].reshape(512, TOK) for n in range(4)], axis=1
                )
                right = xa[arr * 2 + rel, pl.ds(step * 4, 4)].reshape(512, 512)
                total[...] += jnp.dot(left, right, preferred_element_type=F32)

    for stream, steps in SCHEDULE2:
        if stream == "taps":
            arrived(tap_twin)
            fall[row] = fown[...] + fboth[...]

            @pl.loop(1, 16)
            def _(s):
                other = lax.rem(row + s, 16)
                pltpu.make_async_remote_copy(
                    fall.at[row], fall.at[row], tap_send, tap_recv,
                    device_id={"row": other, "col": col, "dp": dp}, device_id_type=MESH,
                ).start()

        elif stream == "outer":
            outer(gat, 0, acc)
            out_ref[...] = acc[...].T
        else:
            run({"h0": h0, "h1": h1, "z2": z2, "g0": g0, "g1": g1}[stream], steps)
    outer(dlv, 1, val_ref)

    pltpu.make_async_copy(fall.at[pl.ds(0, 15)], fall.at[pl.ds(0, 15)], tap_recv).wait()
    for r in range(16):
        tap_ref[pl.ds(2 * r, 2), :] = fall[r, 0:2, :]

    pltpu.make_async_copy(t3.at[pl.ds(0, 15)], t3.at[pl.ds(0, 15)], a2a_send).wait()
    pltpu.make_async_copy(fall.at[pl.ds(0, 15)], fall.at[pl.ds(0, 15)], tap_send).wait()
    for c in copies:
        c.wait_send()


def local(grad_output, block_input, query_branch, key_branch, value_branch, out_weight, filters):
    vmem = pl.BlockSpec(memory_space=pltpu.VMEM)
    hbm = pl.BlockSpec(memory_space=pl.ANY)
    return pl.pallas_call(
        kernel,
        out_shape=(
            jax.ShapeDtypeStruct((512, 512), F32),
            jax.ShapeDtypeStruct((512, 512), F32),
            jax.ShapeDtypeStruct((32, 128), F32),
        ),
        in_specs=[hbm] * 7,
        out_specs=(vmem, vmem, vmem),
        scratch_shapes=[
            pltpu.VMEM((4, BLK, TOK, 512), BF16),
            pltpu.VMEM((3, TOK, 512), BF16),
            pltpu.VMEM((512, 512), BF16),
            pltpu.VMEM((32, 128), F32),
            pltpu.VMEM((512, 512), BF16),
            pltpu.VMEM((BLK, 3, SUB, TOK), BF16),
            pltpu.VMEM((BLK, 3, SUB, TOK), BF16),
            pltpu.VMEM((NX, NY, BLK, SUB, TOK), BF16),
            pltpu.VMEM((NX, NY, BLK, SUB, TOK), BF16),
            pltpu.VMEM((2, 4, NYL, 2, SUB, TOK), RDT),
            pltpu.VMEM((2, 4, NYL, 2, SUB, TOK), RDT),
            pltpu.VMEM((2, 4, NYL, 2, SUB, TOK), F32),
            pltpu.VMEM((2, 4, NYL, 2, SUB, TOK), F32),
            pltpu.VMEM((2, 4, NYL, 2, SUB, TOK), RDT),
            pltpu.VMEM((2, 4, NYL, 2, SUB, TOK), RDT),
            pltpu.VMEM((2, 4, NYL, 2, SUB, TOK), F32),
            pltpu.VMEM((2, 4, 3, 2, SUB, TOK), F32),
            pltpu.VMEM((BLK, SUB, TOK), F32),
            pltpu.VMEM((512, 512), F32),
            pltpu.VMEM((8, 128), F32),
            pltpu.VMEM((8, 128), F32),
            pltpu.VMEM((16, 8, 128), F32),
            pltpu.SemaphoreType.DMA((7,)),
            pltpu.SemaphoreType.DMA,
            pltpu.SemaphoreType.DMA,
            pltpu.SemaphoreType.DMA,
            pltpu.SemaphoreType.DMA,
            pltpu.SemaphoreType.DMA((SEMS,)),
            pltpu.SemaphoreType.DMA((SEMS,)),
        ],
        compiler_params=pltpu.CompilerParams(collective_id=0, has_side_effects=True, vmem_limit_bytes=60 * 1024 * 1024),
    )(grad_output, block_input, query_branch, key_branch, value_branch, out_weight, filters)


def solution(mesh):
    in_specs = (
        P("dp", "col", "row"),
        P("dp", "col", "row"),
        P("dp", "row", "col"),
        P("dp", "row", "col"),
        P("dp", "row", "col"),
        P("row", "col"),
        P("col", None),
    )
    out_specs = (P("row", "col"), P("col", "row"), P("col", None))
    return jax.shard_map(local, mesh=mesh, in_specs=in_specs, out_specs=out_specs, check_vma=False)
```

time: 173 us -> 130 us (0.75)
  the two profiles are of different devices: /device:TPU:8 before, /device:TPU:2 now
where the time goes in v2:
time: 130 us
  Pallas kernels  125 us (96%)
  local copies, waits for them, and re-layouts  3.93 us (3%)
    pallas_call x1, Pallas kernels, local(): pl.pallas_call(kernel, out_shape=(jax.ShapeDtypeStruct((512, 512), F32),...  125 us
    unnamed x7, local copies, waits for them, and re-layouts  3.93 us

profile of v2, /device:TPU:2, one launch (start us, length us, event | category | flops | bytes accessed | tf_op | source)
XLA Modules:
  0.0 129.6 jit_solution(1279295084393453537)
XLA Ops:
  0.6 125.0 %shard_map.94 = (f32[512,512]{1,0:T(8,128)}, f32[512,512]{1,0:T(8,128)}, f32[32,128]{1,0:T(8,128)}) custom-call(bf16[1,128,512]{2,1,0:T(8,128)(2,1)} %g_hbm.1, bf16[1,128,512]{2,1,0:T(8,128)(2,1)} %i_hbm.1, bf16[1,128,512]{2,1,0:T(8,128)(2,1)} %q_hbm.1, bf16[1,128,512]{2,1,0:T(8,128)(2,1)} %k_hbm.1, bf16[1,128,512]{2,1,0:T(8,128)(2,1)} %v_hbm.1, ...), custom_call_target="tpu_custom_call" | custom-call | tf_op jit(solution)/shard_map/pallas_call | solution.py:445
  125.7 0.0 copy-start
  125.7 2.4 %copy.13 = f32[512,512]{1,0:T(8,128)} copy(f32[512,512]{1,0:T(8,128)} %get-tuple-element.6) | data formatting | bytes 2097152
  128.0 0.0 copy-done
  128.0 0.0 copy-start.1
  128.0 1.0 copy.14
  129.0 0.0 copy-done.1
  129.0 0.6 copy.15
Async XLA Ops:
  125.7 2.4 %copy-start = (f32[512,512]{1,0:T(8,128)S(1)}, f32[512,512]{1,0:T(8,128)}, u32[]{:S(2)}) copy-start(f32[512,512]{1,0:T(8,128)} %get-tuple-element.7) | copy-start | bytes 3145732
  128.0 1.0 copy-start.1

commit v3 on v2

--- a/solution.py
+++ b/solution.py
@@ -14,16 +14,11 @@
 SUB = 32
 SEMS = 220
 AG1 = (10, ((10, 3), (13, 3)))
-AG2 = (9, ((9, 4), (13, 3)))
-SCHEDULE1 = (
-    ("cross", 1), ("late", 3), ("cross", 2), ("cross", 3), ("h0", 1), ("h1", 1), ("h0", 1),
-    ("finish", 0), ("finish", 1), ("finish", 2), ("z2", 1), ("finish", 3),
-)
-SCHEDULE2 = (
-    ("g1", 1), ("g0", 1), ("h0", 1), ("h1", 1), ("g0", 1), ("g1", 1), ("h0", 2), ("z2", 1), ("g0", 1), ("h1", 2), ("z2", 1), ("g0", 1), ("g1", 2), ("h0", 1), ("h1", 2), ("taps", 0),
-    ("z2", 1), ("g0", 2), ("z2", 1), ("g1", 2), ("h1", 9), ("g0", 2), ("h0", 9), ("z2", 99), ("outer", 0), ("g1", 2), ("g0", 99), ("g1", 99),
-)
+AG2 = (10, ((10, 3), (13, 3)))
+SCHEDULE1 = (("cross", 1), ("late", 3), ("cross", 2), ("cross", 3), ("h0", 1), ("h1", 1), ("h0", 1), ("finish", 0), ("finish", 1), ("finish", 2), ("z2", 1), ("finish", 3),)
+SCHEDULE2 = (("g1", 1), ("g0", 1), ("h0", 1), ("h1", 1), ("g0", 1), ("g1", 1), ("h0", 2), ("z2", 1), ("g0", 1), ("h1", 2), ("z2", 1), ("g0", 1), ("g1", 2), ("h0", 1), ("h1", 2), ("taps", 0), ("z2", 1), ("g0", 2), ("z2", 1), ("g1", 2), ("h1", 9), ("g0", 2), ("h0", 9), ("z2", 99), ("outer", 0), ("g1", 2), ("g0", 99), ("g1", 99),)
 RDT = BF16
+NARROW = (2,)
 
 
 def exact_dot(a, b, dims):
@@ -42,7 +37,7 @@
 def kernel(
     g_hbm, i_hbm, q_hbm, k_hbm, v_hbm, w_hbm, f_hbm,
     out_ref, val_ref, tap_ref,
-    xa, tok, w_ref, f_ref, wt, t3, qkv, gat, dlv, far_out, near_out, late_out, own_sum, r1, r2n, r2l, ry, dsum, acc, fown, fboth, fall,
+    xa, tok, w_ref, f_ref, wt, t3, qkv, gat, dlv, far_out, near_out, late_out, own_sum, r1, r2n, r2l, own_b, ryb, ry, dsum, acc, fown, fboth, fall,
     loc_sem, a2a_send, a2a_recv, tap_send, tap_recv, send_sem, recv_sem,
 ):
     row, col, dp = lax.axis_index("row"), lax.axis_index("col"), lax.axis_index("dp")
@@ -307,14 +302,18 @@
         arrived(*near[p], *late[p])
         for half in range(2):
             own_sum[half, p] = own_sum[half, p] + (r2n[half, p].astype(F32) + r2l[half, p])
+            if NARROW:
+                own_b[half, p] = own_sum[half, p].astype(BF16)
             for d in range(1, 4):
                 peer = lax.rem(YL + d, NYL)
-                cross[half, p, d] = send(own_sum.at[half, p, peer], ry.at[half, p, d - 1], at(X, dp * NYL + peer, Z, K))
+                src, dst = (own_b, ryb) if d in NARROW else (own_sum, ry)
+                cross[half, p, d] = send(src.at[half, p, peer], dst.at[half, p, d - 1], at(X, dp * NYL + peer, Z, K))
 
     def finish(p):
         for half in range(2):
             arrived(*[cross[half, p, d] for d in range(1, 4)])
-            total = own_sum[half, p, YL] + ((ry[half, p, 0] + ry[half, p, 1]) + ry[half, p, 2])
+            terms = [(ryb if d in NARROW else ry)[half, p, d - 1].astype(F32) for d in range(1, 4)]
+            total = own_sum[half, p, YL] + ((terms[0] + terms[1]) + terms[2])
             dsum[pl.ds(wz(offsets[half][p]) * 2, 2)] = total
 
     z1 = gather_first()
@@ -468,6 +467,8 @@
             pltpu.VMEM((2, 4, NYL, 2, SUB, TOK), RDT),
             pltpu.VMEM((2, 4, NYL, 2, SUB, TOK), RDT),
             pltpu.VMEM((2, 4, NYL, 2, SUB, TOK), F32),
+            pltpu.VMEM((2, 4, NYL, 2, SUB, TOK), BF16),
+            pltpu.VMEM((2, 4, 3, 2, SUB, TOK), BF16),
             pltpu.VMEM((2, 4, 3, 2, SUB, TOK), F32),
             pltpu.VMEM((BLK, SUB, TOK), F32),
             pltpu.VMEM((512, 512), F32),

time: 130 us -> 124 us (0.954)
  the two profiles are of different devices: /device:TPU:2 before, /device:TPU:64 now
where the time goes in v3:
time: 124 us
  Pallas kernels  120 us (97%)
  local copies, waits for them, and re-layouts  3.93 us (3%)
    pallas_call x1, Pallas kernels, local(): pl.pallas_call(kernel, out_shape=(jax.ShapeDtypeStruct((512, 512), F32),...  120 us
    unnamed x7, local copies, waits for them, and re-layouts  3.93 us

profile of v3, /device:TPU:64, one launch (start us, length us, event | category | flops | bytes accessed | tf_op | source)
XLA Modules:
  0.0 124.3 jit_solution(5150908604553970509)
XLA Ops:
  0.6 119.7 %shard_map.94 = (f32[512,512]{1,0:T(8,128)}, f32[512,512]{1,0:T(8,128)}, f32[32,128]{1,0:T(8,128)}) custom-call(bf16[1,128,512]{2,1,0:T(8,128)(2,1)} %g_hbm.1, bf16[1,128,512]{2,1,0:T(8,128)(2,1)} %i_hbm.1, bf16[1,128,512]{2,1,0:T(8,128)(2,1)} %q_hbm.1, bf16[1,128,512]{2,1,0:T(8,128)(2,1)} %k_hbm.1, bf16[1,128,512]{2,1,0:T(8,128)(2,1)} %v_hbm.1, ...), custom_call_target="tpu_custom_call" | custom-call | tf_op jit(solution)/shard_map/pallas_call | solution.py:444
  120.3 0.0 copy-start
  120.3 2.4 %copy.13 = f32[512,512]{1,0:T(8,128)} copy(f32[512,512]{1,0:T(8,128)} %get-tuple-element.6) | data formatting | bytes 2097152
  122.7 0.0 copy-done
  122.7 0.0 copy-start.1
  122.7 1.0 copy.14
  123.7 0.0 copy-done.1
  123.7 0.6 copy.15
Async XLA Ops:
  120.3 2.4 %copy-start = (f32[512,512]{1,0:T(8,128)S(1)}, f32[512,512]{1,0:T(8,128)}, u32[]{:S(2)}) copy-start(f32[512,512]{1,0:T(8,128)} %get-tuple-element.7) | copy-start | bytes 3145732
  122.7 1.0 copy-start.1

commit v4 on v3

--- a/solution.py
+++ b/solution.py
@@ -16,7 +16,7 @@
 AG1 = (10, ((10, 3), (13, 3)))
 AG2 = (10, ((10, 3), (13, 3)))
 SCHEDULE1 = (("cross", 1), ("late", 3), ("cross", 2), ("cross", 3), ("h0", 1), ("h1", 1), ("h0", 1), ("finish", 0), ("finish", 1), ("finish", 2), ("z2", 1), ("finish", 3),)
-SCHEDULE2 = (("g1", 1), ("g0", 1), ("h0", 1), ("h1", 1), ("g0", 1), ("g1", 1), ("h0", 2), ("z2", 1), ("g0", 1), ("h1", 2), ("z2", 1), ("g0", 1), ("g1", 2), ("h0", 1), ("h1", 2), ("taps", 0), ("z2", 1), ("g0", 2), ("z2", 1), ("g1", 2), ("h1", 9), ("g0", 2), ("h0", 9), ("z2", 99), ("outer", 0), ("g1", 2), ("g0", 99), ("g1", 99),)
+SCHEDULE2 = (("g1", 1), ("g0", 1), ("h0", 1), ("h1", 1), ("g0", 1), ("g1", 1), ("h0", 2), ("z2", 1), ("g0", 1), ("h1", 2), ("z2", 1), ("g0", 1), ("g1", 2), ("h0", 1), ("h1", 2), ("taps", 0), ("z2", 1), ("g0", 2), ("z2", 1), ("g1", 2), ("h1", 2), ("g0", 2), ("g1", 2), ("h1", 9), ("g0", 1), ("h0", 9), ("z2", 99), ("outer", 0), ("g0", 99), ("g1", 99),)
 RDT = BF16
 NARROW = (2,)
 
@@ -57,6 +57,7 @@
         return lax.rem(Z + (d + NZ), NZ)
 
     xp, xm = at(wx(1), Y, Z, K), at(wx(-1), Y, Z, K)
+    xfar = at(wx(2), Y, Z, K)
     yp, ym = at(X, wy(1), Z, K), at(X, wy(-1), Z, K)
     zp, zm = at(X, Y, wz(1), K), at(X, Y, wz(-1), K)
     mate = at(X, Y, Z, 1 - K)
@@ -93,17 +94,13 @@
         c.start()
 
     barrier = pltpu.get_barrier_semaphore()
-    me = row * 2 + dp
-
-    def group_peer(s):
-        other = lax.rem(me + s, 32)
-        return {"row": lax.div(other, 2), "col": col, "dp": lax.rem(other, 2)}
-
-    @pl.loop(1, 32)
+
+    @pl.loop(1, 16)
     def _(s):
-        pl.semaphore_signal(barrier, inc=1, device_id=group_peer(s), device_id_type=MESH)
-
-    for other in (zp, zm, mate):
+        peer = {"row": lax.rem(row + s, 16), "col": col, "dp": dp}
+        pl.semaphore_signal(barrier, inc=1, device_id=peer, device_id_type=MESH)
+
+    for other in (twin, yp, ym, zp, zm, mate):
         pl.semaphore_signal(barrier, inc=1, device_id=other, device_id_type=MESH)
 
     at_s = lax.broadcasted_iota(jnp.int32, (TOK, TOK), 0)
@@ -120,7 +117,7 @@
         taps = jnp.broadcast_to(f_ref[pl.ds(row * 2 + grp, 1), :], (TOK, TOK))
         wrapped = skew(taps, False)
         tables.append((jnp.where(same, wrapped, 0.0), jnp.where(same, 0.0, wrapped)))
-    pl.semaphore_wait(barrier, 34)
+    pl.semaphore_wait(barrier, 21)
 
     mates = {}
 
@@ -236,7 +233,6 @@
 
     def x_first(buf, n0, subs):
         n1 = BLK - n0
-        h = n1 // 2
 
         def one(x, lo=0, n=n1):
             return buf.at[x, Y, pl.ds(n0 + lo, n)]
@@ -246,11 +242,10 @@
             return buf.at[pl.ds(lo, n), wy(o), pl.ds(first, count)]
 
         b = both(one(X), one(X), xp, xm)
-        yield
-        arrived(*b)
-        b = both(one(wx(-1), 0, h), one(wx(1), h, n1 - h), xp, xm)
-        yield
-        arrived(*b)
+        c = send(one(X), one(X), xfar)
+        yield
+        yield
+        arrived(*b, c)
         rings = [both(rows_of(0, n), rows_of(0, n), yp, ym) for n in range(len(subs))]
         yield
         for o in (1, 2, 3):

time: 124 us -> 122 us (0.984)
  the two profiles are of different devices: /device:TPU:64 before, /device:TPU:8 now
where the time goes in v4:
time: 122 us
  Pallas kernels  118 us (97%)
  local copies, waits for them, and re-layouts  3.93 us (3%)
    pallas_call x1, Pallas kernels, local(): pl.pallas_call(kernel, out_shape=(jax.ShapeDtypeStruct((512, 512), F32),...  118 us
    unnamed x7, local copies, waits for them, and re-layouts  3.93 us

profile of v4, /device:TPU:8, one launch (start us, length us, event | category | flops | bytes accessed | tf_op | source)
XLA Modules:
  0.0 122.1 jit_solution(9833319445733325886)
XLA Ops:
  0.6 117.6 %shard_map.94 = (f32[512,512]{1,0:T(8,128)}, f32[512,512]{1,0:T(8,128)}, f32[32,128]{1,0:T(8,128)}) custom-call(bf16[1,128,512]{2,1,0:T(8,128)(2,1)} %g_hbm.1, bf16[1,128,512]{2,1,0:T(8,128)(2,1)} %i_hbm.1, bf16[1,128,512]{2,1,0:T(8,128)(2,1)} %q_hbm.1, bf16[1,128,512]{2,1,0:T(8,128)(2,1)} %k_hbm.1, bf16[1,128,512]{2,1,0:T(8,128)(2,1)} %v_hbm.1, ...), custom_call_target="tpu_custom_call" | custom-call | tf_op jit(solution)/shard_map/pallas_call | solution.py:439
  118.2 0.0 copy-start
  118.2 2.4 %copy.13 = f32[512,512]{1,0:T(8,128)} copy(f32[512,512]{1,0:T(8,128)} %get-tuple-element.6) | data formatting | bytes 2097152
  120.6 0.0 copy-done
  120.6 0.0 copy-start.1
  120.6 1.0 copy.14
  121.5 0.0 copy-done.1
  121.5 0.6 copy.15
Async XLA Ops:
  118.2 2.4 %copy-start = (f32[512,512]{1,0:T(8,128)S(1)}, f32[512,512]{1,0:T(8,128)}, u32[]{:S(2)}) copy-start(f32[512,512]{1,0:T(8,128)} %get-tuple-element.7) | copy-start | bytes 3145732
  120.6 1.0 copy-start.1

commit v5 on v4

--- a/solution.py
+++ b/solution.py
@@ -260,8 +260,8 @@
             arrived(*rings[n])
 
     offsets = ((0, -1, -2, -3), (1, 2, 3, 4))
-    far = [None] * 4
-    near = [None] * 4
+    far = [[None, None] for _ in range(4)]
+    near = [[None, None] for _ in range(4)]
     late = [None] * 4
     cross = {}
 
@@ -272,18 +272,18 @@
         for n in range(2):
             out[half, p, :, n] = res[:, n * TOK : (n + 1) * TOK].reshape(NYL, SUB, TOK).astype(out.dtype)
 
+    def start_half(p, half):
+        arrived(mates[offsets[half][p]])
+        product(2, half, p, far_out)
+        far[p][half] = send(far_out.at[half, p], r1.at[half, p], (xp, xm)[half])
+        product((3, 1)[half], half, p, near_out)
+        near[p][half] = send(near_out.at[half, p], r2n.at[half, p], (xm, xp)[half])
+        product((1, 3)[half], half, p, late_out)
+        product(0, half, p, own_sum)
+
     def start_piece(p):
-        arrived(mates[offsets[0][p]], mates[offsets[1][p]])
-        product(2, 0, p, far_out)
-        product(2, 1, p, far_out)
-        far[p] = (send(far_out.at[0, p], r1.at[0, p], xp), send(far_out.at[1, p], r1.at[1, p], xm))
-        product(1, 1, p, near_out)
-        product(3, 0, p, near_out)
-        near[p] = (send(near_out.at[1, p], r2n.at[1, p], xp), send(near_out.at[0, p], r2n.at[0, p], xm))
-        product(1, 0, p, late_out)
-        product(3, 1, p, late_out)
-        product(0, 0, p, own_sum)
-        product(0, 1, p, own_sum)
+        start_half(p, 0)
+        start_half(p, 1)
 
     def start_late(p):
         sent = []
@@ -324,8 +324,9 @@
 
     tw_g = send(xa.at[0, col], xa.at[1, col], twin)
     tw_i = send(xa.at[2, col], xa.at[3, col], twin)
+    start_half(0, 0)
     run(z1, 1)
-    start_piece(0)
+    start_half(0, 1)
     run(z1, 1)
     start_piece(1)
     start_late(0)

time: 122 us -> 121 us (level)
  no operation moved by 1% of the time
where the time goes in v5:
time: 121 us
  Pallas kernels  117 us (97%)
  local copies, waits for them, and re-layouts  3.93 us (3%)
    pallas_call x1, Pallas kernels, local(): pl.pallas_call(kernel, out_shape=(jax.ShapeDtypeStruct((512, 512), F32),...  117 us
    unnamed x7, local copies, waits for them, and re-layouts  3.93 us

profile of v5, /device:TPU:8, one launch (start us, length us, event | category | flops | bytes accessed | tf_op | source)
XLA Modules:
  0.0 121.2 jit_solution(13895008645706355952)
XLA Ops:
  0.6 116.6 %shard_map.94 = (f32[512,512]{1,0:T(8,128)}, f32[512,512]{1,0:T(8,128)}, f32[32,128]{1,0:T(8,128)}) custom-call(bf16[1,128,512]{2,1,0:T(8,128)(2,1)} %g_hbm.1, bf16[1,128,512]{2,1,0:T(8,128)(2,1)} %i_hbm.1, bf16[1,128,512]{2,1,0:T(8,128)(2,1)} %q_hbm.1, bf16[1,128,512]{2,1,0:T(8,128)(2,1)} %k_hbm.1, bf16[1,128,512]{2,1,0:T(8,128)(2,1)} %v_hbm.1, ...), custom_call_target="tpu_custom_call" | custom-call | tf_op jit(solution)/shard_map/pallas_call | solution.py:440
  117.3 0.0 copy-start
  117.3 2.4 %copy.13 = f32[512,512]{1,0:T(8,128)} copy(f32[512,512]{1,0:T(8,128)} %get-tuple-element.6) | data formatting | bytes 2097152
  119.6 0.0 copy-done
  119.6 0.0 copy-start.1
  119.6 1.0 copy.14
  120.6 0.0 copy-done.1
  120.6 0.6 copy.15
Async XLA Ops:
  117.3 2.4 %copy-start = (f32[512,512]{1,0:T(8,128)S(1)}, f32[512,512]{1,0:T(8,128)}, u32[]{:S(2)}) copy-start(f32[512,512]{1,0:T(8,128)} %get-tuple-element.7) | copy-start | bytes 3145732
  119.6 1.0 copy-start.1
